TPU v7x, 32 devices: a whole 2x2x4 slice. The times are simulated.
32 devices in a mesh: dp: 8 (over z, x), mp: 4 (over y, core).
Axes of the slice: x: 2, y: 2, z: 4, core: 2. Of those that a mesh axis runs over, the one named last changes fastest.
Arguments:
- activations: bfloat16 [4096, 3072], P('dp', 'mp'), may hold values from -6 to 6
- out_grads: bfloat16 [4096, 6144], P('dp', 'mp'), may hold values from -0.25 to 0.25
- error: bfloat16 [8, 3072, 6144], P('dp', 'mp'), may hold values from -8 to 8
- sketch: bfloat16 [6144, 64], replicated, may hold values from -0.078125 to 0.078125
- momentum: float32 [3072, 6144], P('mp', 'dp'), may hold values from -6 to 6
Outputs:
- error_new: bfloat16 [8, 3072, 6144], P('dp', 'mp')
- momentum_new: float32 [3072, 6144], P('mp', 'dp')
- next_sketch: bfloat16 [6144, 64], replicated
All inputs are finite; a program needn't handle non-finite values.
Results may differ from a plain program's by a relative error of at most 0.0057.
Values may be sent and summed in bfloat16 or wider, within the bound.
A program may use at most 64 MiB of HBM per device.

v0:
```python
import jax
import jax.numpy as jnp
from jax import lax
from jax.sharding import PartitionSpec as P

beta_decay = 0.9


def update_momentum(momentum, basis_rows, sketch_block):
    product = lax.dot_general(
        basis_rows, sketch_block, (((1,), (1,)), ((), ())), preferred_element_type=jnp.float32
    )
    return beta_decay * momentum + product


def local(activations, out_grads, error, sketch, momentum):
    own_error = error[0]
    product = lax.dot_general(
        activations,
        lax.all_gather(out_grads, "mp", axis=1, tiled=True),
        (((0,), (0,)), ((), ())),
        preferred_element_type=jnp.float32,
    )
    accumulated = (product + own_error.astype(jnp.float32)).astype(jnp.bfloat16)
    local_left = jnp.dot(accumulated, sketch, preferred_element_type=jnp.float32)
    left_sketch = lax.psum(local_left, "dp")
    gram_local = jnp.dot(
        left_sketch.T,
        left_sketch,
        precision=lax.Precision.HIGHEST,
        preferred_element_type=jnp.float32,
    )
    gram_matrix = lax.psum(gram_local, "mp")
    factor = jnp.linalg.cholesky(gram_matrix)
    basis_rows = jax.scipy.linalg.solve_triangular(factor, left_sketch.T, lower=True).T.astype(
        jnp.bfloat16
    )
    block_width = momentum.shape[1]
    local_right = lax.dot_general(
        accumulated, basis_rows, (((0,), (0,)), ((), ())), preferred_element_type=jnp.float32
    )
    right_sketch = lax.psum(local_right, ("dp", "mp"))
    next_sketch = right_sketch.astype(jnp.bfloat16)
    sketch_part = lax.dynamic_slice_in_dim(
        next_sketch, lax.axis_index("dp") * block_width, block_width, 0
    )
    momentum_new = update_momentum(momentum, basis_rows, sketch_part)
    decoded = lax.dot_general(
        basis_rows, next_sketch, (((1,), (1,)), ((), ())), preferred_element_type=jnp.float32
    )
    error_new = (accumulated.astype(jnp.float32) - decoded / lax.axis_size("dp")).astype(
        jnp.bfloat16
    )
    return (error_new[None], momentum_new, next_sketch)


def solution(mesh):
    in_specs = (P("dp", "mp"), P("dp", "mp"), P("dp", "mp", None), P(), P("mp", "dp"))
    out_specs = (P("dp", "mp", None), P("mp", "dp"), P())
    return jax.shard_map(local, mesh=mesh, in_specs=in_specs, out_specs=out_specs, check_vma=False)
```

profile of v0, /device:TPU:0, one launch (start us, length us, event | category | flops | bytes accessed | tf_op | source)
XLA Modules:
  0.0 249.4 jit_solution(14047941913646381180)
XLA Ops:
  7.2 0.0 copy-start
  7.2 0.0 all-gather.2.cloned.1.call-start
  7.2 0.7 all-gather.2.cloned.1.call-update
  7.9 0.0 copy-start.4
  7.9 0.0 all-reduce.3.cloned.1.call-start
  8.0 50.7 %all-gather.2.cloned.1.call-done = bf16[512,6144]{1,0:T(8,128)(2,1)} async-done(((bf16[512,1536]{1,0:T(8,128)(2,1)}), bf16[512,6144]{1,0:T(8,128)(2,1)}) %all-gather.2.cloned.1.call-update) | async-done | bytes 6291472 | tf_op jit(solution)/shard_map/all_gather | solution.py:20
  58.7 0.0 copy-done
  58.7 9.6 %fusion = bf16[768,6144]{1,0:T(8,128)(2,1)S(1)} fusion(bf16[1,768,6144]{2,1,0:T(8,128)(2,1)} %param.7, bf16[512,768]{1,0:T(8,128)(2,1)S(1)} %copy-done, bf16[512,6144]{1,0:T(8,128)(2,1)} %all-gather.2.cloned.1.call-done), kind=kOutput, calls=%fused_computation.1 | convolution fusion | flops 4845993984 | bytes 25952256 | tf_op jit(solution)/shard_map/dot_general | solution.py:18
  68.3 0.0 copy-start.1
  68.3 3.7 %copy-done.1 = bf16[768,6144]{1,0:T(8,128)(2,1)} copy-done((bf16[768,6144]{1,0:T(8,128)(2,1)}, bf16[768,6144]{1,0:T(8,128)(2,1)S(1)}, u32[]{:S(2)}) %copy-start.1) | copy-done | bytes 9437208
  72.1 0.0 copy-done.4
  72.1 3.7 %fusion.7 = f32[768,64]{0,1:T(8,128)} fusion(bf16[768,6144]{1,0:T(8,128)(2,1)S(1)} %fusion, bf16[6144,64]{0,1:T(8,128)(2,1)S(1)} %copy-done.4), kind=kOutput, calls=%fused_computation.17 | convolution fusion | flops 603979776 | bytes 10420224 | tf_op jit(solution)/shard_map/dot_general | solution.py:25
  75.7 0.0 all-reduce.3.cloned.1.call-update
  75.8 70.8 %all-reduce.3.cloned.1.call-done = f32[768,64]{0,1:T(8,128)} async-done(((f32[768,64]{0,1:T(8,128)}), f32[768,64]{0,1:T(8,128)}) %all-reduce.3.cloned.1.call-update) | async-done | bytes 196624 | tf_op jit(solution)/shard_map/psum | solution.py:26
  146.6 1.3 fusion.8
  147.9 10.3 %psum.22 = f32[64,64]{0,1:T(8,128)S(1)} all-reduce(f32[64,64]{0,1:T(8,128)S(1)} %fusion.8), channel_id=1, replica_groups=mesh['dp'=8,'mp'=4] {'mp'}, use_global_device_ids=true, to_apply=%region_1.0 | all-reduce | flops 4096 | bytes 32768 | tf_op jit(solution)/shard_map/psum | solution.py:33
  158.2 0.1 copy.9
  158.3 5.8 %cholesky.16 = f32[64,64]{1,0:T(8,128)S(1)} custom-call(f32[64,64]{1,0:T(8,128)S(1)} %fusion.5), custom_call_target="Cholesky" | custom-call | tf_op jit(solution)/shard_map/jit(cholesky)/cholesky | solution.py:34
  164.2 0.6 compare_reduce_fusion
  164.8 0.7 fusion.3
  165.5 4.9 %custom-call.7 = f32[1,64,64]{1,2,0:T(8,128)S(1)} custom-call(f32[1,64,64]{2,1,0:T(8,128)S(1)} %fusion.3), custom_call_target="InvertDiagBlocksLowerTriangular" | custom-call | tf_op jit(solution)/shard_map/jit(_solve_triangular)/triangular_solve | solution.py:35
  170.4 1.3 convolution_convert_fusion
  171.7 5.4 %fusion.9 = f32[6144,64]{0,1:T(8,128)S(1)} fusion(bf16[768,64]{0,1:T(8,128)(2,1)S(1)} %convolution_convert_fusion, bf16[768,6144]{1,0:T(8,128)(2,1)} %copy-done.1), kind=kOutput, calls=%fused_computation.19 | convolution fusion | flops 603979776 | bytes 11108352 | tf_op jit(solution)/shard_map/dot_general | solution.py:39
  177.1 55.7 %all-reduce.4 = bf16[6144,64]{0,1:T(8,128)(2,1)S(1)} all-reduce(f32[6144,64]{0,1:T(8,128)S(1)} %fusion.9), channel_id=1, replica_groups=mesh['dp'=8,'mp'=4] {'dp','mp'}, use_global_device_ids=true, to_apply=%region_4.5 | all-reduce | flops 393216 | bytes 2359296 | tf_op jit(solution)/shard_map/psum | solution.py:42
  232.8 0.0 copy-start.2
  232.8 0.0 copy-start.3
  232.8 7.8 %fusion.1 = bf16[1,768,6144]{2,1,0:T(8,128)(2,1)} fusion(bf16[768,64]{0,1:T(8,128)(2,1)S(1)} %convolution_convert_fusion, bf16[6144,64]{0,1:T(8,128)(2,1)S(1)} %all-reduce.4, bf16[768,6144]{1,0:T(8,128)(2,1)} %copy-done.1), kind=kOutput, calls=%fused_computation.3 | convolution fusion | flops 622854144 | bytes 19759104 | tf_op jit(solution)/shard_map/dot_general | solution.py:48
  240.7 0.0 copy-done.2
  240.7 0.0 copy-done.3
  240.7 1.9 multiply_add_fusion
  (2 shorter events, 0.0 us)
Async XLA Ops:
  7.2 51.5 %copy-start = (bf16[512,768]{1,0:T(8,128)(2,1)S(1)}, bf16[512,768]{1,0:T(8,128)(2,1)}, u32[]{:S(2)}) copy-start(bf16[512,768]{1,0:T(8,128)(2,1)} %param.5) | copy-start | bytes 2359300
  7.2 51.5 %all-gather.2.cloned.1.call-start = ((), (), s32[]{:S(2)}) async-start(), calls=%async_computation | async-start | bytes 7864320 | tf_op jit(solution)/shard_map/all_gather | solution.py:20
  7.9 64.2 %copy-start.4 = (bf16[6144,64]{0,1:T(8,128)(2,1)S(1)}, bf16[6144,64]{0,1:T(8,128)(2,1)}, u32[]{:S(2)}) copy-start(bf16[6144,64]{0,1:T(8,128)(2,1)} %param.8) | copy-start | bytes 2359300
  7.9 138.7 %all-reduce.3.cloned.1.call-start = ((), (), s32[]{:S(2)}) async-start(), calls=%async_computation.1 | async-start | bytes 393216 | tf_op jit(solution)/shard_map/psum | solution.py:26
  68.3 3.7 %copy-start.1 = (bf16[768,6144]{1,0:T(8,128)(2,1)}, bf16[768,6144]{1,0:T(8,128)(2,1)S(1)}, u32[]{:S(2)}) copy-start(bf16[768,6144]{1,0:T(8,128)(2,1)S(1)} %fusion) | copy-start | bytes 28311556
  232.8 7.8 %copy-start.2 = (bf16[6144,64]{0,1:T(8,128)(2,1)}, bf16[6144,64]{0,1:T(8,128)(2,1)S(1)}, u32[]{:S(2)}) copy-start(bf16[6144,64]{0,1:T(8,128)(2,1)S(1)} %all-reduce.4) | copy-start | bytes 2359300
  232.8 7.8 %copy-start.3 = (f32[768,768]{1,0:T(8,128)S(1)}, f32[768,768]{1,0:T(8,128)}, u32[]{:S(2)}) copy-start(f32[768,768]{1,0:T(8,128)} %param.9) | copy-start | bytes 7077892
Sparse Core Ops, SparseCore 0:
  9.5 49.0 all-gather.1
  75.9 70.6 all-reduce.2
where the time goes:
time: 250 us; the launch traced here: 249 us
  waiting for transfers between devices  122 us (49%)
  blocking collectives  66 us (26%)
  matrix products  31.1 us (12%)
  between operations  14.2 us (6%)
  other arithmetic  12.1 us (5%)
  local copies, waits for them, and re-layouts  3.84 us (2%)
    psum x1, waiting for transfers between devices, local(): left_sketch = lax.psum(local_left, 'dp')  70.8 us
    psum x1, blocking collectives, local(): right_sketch = lax.psum(local_right, ('dp', 'mp'))  55.7 us
    all_gather x1, waiting for transfers between devices, local(): lax.all_gather(out_grads, 'mp', axis=1, tiled=True)  50.7 us
    psum x1, blocking collectives, local(): gram_matrix = lax.psum(gram_local, 'mp')  10.3 us
    dot_general x1, matrix products, local(): lax.dot_general(activations, lax.all_gather(out_grads, 'mp', axis=1, tile...  9.64 us
    dot_general x1, matrix products, local(): lax.dot_general(basis_rows, next_sketch, (((1,), (1,)), ((), ())), prefer...  7.81 us
    another operation x3, other arithmetic, local(): factor = jnp.linalg.cholesky(gram_matrix)  6.52 us
    another operation x2, other arithmetic, local(): jax.scipy.linalg.solve_triangular(factor, left_sketch.T, lower=True)  5.55 us
  transfers between devices with their start and end apart: 2, of which 2 were waited for; matrix products, arithmetic and copies ran while one was open for 0% of the time, Pallas kernels for 0%

commit v1 on v0

--- a/solution.py
+++ b/solution.py
@@ -4,6 +4,13 @@
 from jax.sharding import PartitionSpec as P
 
 beta_decay = 0.9
+
+
+def gather_over(x, name, dim):
+    peers = lax.axis_size(name)
+    pieces = jnp.stack([x for _ in range(peers)])
+    pieces = lax.all_to_all(pieces, name, split_axis=0, concat_axis=0)
+    return jnp.concatenate(pieces, axis=dim)
 
 
 def update_momentum(momentum, basis_rows, sketch_block):
@@ -17,7 +24,7 @@
     own_error = error[0]
     product = lax.dot_general(
         activations,
-        lax.all_gather(out_grads, "mp", axis=1, tiled=True),
+        gather_over(out_grads, "mp", 1),
         (((0,), (0,)), ((), ())),
         preferred_element_type=jnp.float32,
     )

time: 250 us -> 277 us (1.11)
  blocking collectives: 66 us -> 141 us
  waiting for transfers between devices: 122 us -> 71.9 us
    all_to_all x0 -> x1, blocking collectives: none -> 74.9 us  [gather_over(): pieces = lax.all_to_all(pieces, name, split_axis=0, concat_axis=0)]
    all_gather x1 -> x0, waiting for transfers between devices: 50.7 us -> none  [local(): lax.all_gather(out_grads, 'mp', axis=1, tiled=True)]
    unnamed x10 -> x11, local copies, waits for them, and re-layouts: 3.76 us -> 5.54 us
  transfers between devices with their start and end apart: 2 -> 1, of which waited for: 2 -> 1; matrix products, arithmetic and copies ran while one was open for 0% -> 0% of each run, Pallas kernels for 0% -> 0%
where the time goes in v1:
time: 277 us
  blocking collectives  141 us (51%)
  waiting for transfers between devices  71.9 us (26%)
  matrix products  31.2 us (11%)
  between operations  14.2 us (5%)
  other arithmetic  12.1 us (4%)
  local copies, waits for them, and re-layouts  6.11 us (2%)
    all_to_all x1, blocking collectives, gather_over(): pieces = lax.all_to_all(pieces, name, split_axis=0, concat_axis=0)  74.9 us
    psum x1, waiting for transfers between devices, local(): left_sketch = lax.psum(local_left, 'dp')  71.9 us
    psum x1, blocking collectives, local(): right_sketch = lax.psum(local_right, ('dp', 'mp'))  55.9 us
    psum x1, blocking collectives, local(): gram_matrix = lax.psum(gram_local, 'mp')  10.3 us
    dot_general x1, matrix products, local(): lax.dot_general(activations, gather_over(out_grads, 'mp', 1), (((0,), (0,...  9.81 us
    dot_general x1, matrix products, local(): lax.dot_general(basis_rows, next_sketch, (((1,), (1,)), ((), ())), prefer...  7.82 us
    another operation x3, other arithmetic, local(): factor = jnp.linalg.cholesky(gram_matrix)  6.52 us
    another operation x2, other arithmetic, local(): jax.scipy.linalg.solve_triangular(factor, left_sketch.T, lower=True)  5.55 us
  transfers between devices with their start and end apart: 1, of which 1 were waited for; matrix products, arithmetic and copies ran while one was open for 0% of the time, Pallas kernels for 0%

profile of v1, /device:TPU:0, one launch (start us, length us, event | category | flops | bytes accessed | tf_op | source)
XLA Modules:
  0.0 276.5 jit_solution(12735940451821131783)
XLA Ops:
  7.2 0.0 copy-start
  7.2 0.0 all-reduce.3.cloned.1.call-start
  7.2 1.8 copy.10
  9.0 0.5 stack.2
  9.5 74.9 %all_to_all.5 = bf16[4,512,1536]{1,2,0:T(8,128)(2,1)} all-to-all(bf16[4,512,1536]{1,2,0:T(8,128)(2,1)S(1)} %stack.2), channel_id=1, replica_groups=mesh['dp'=8,'mp'=4] {'mp'}, dimensions={0} | all-to-all | bytes 12582912 | tf_op jit(solution)/shard_map/all_to_all | solution.py:12
  84.4 0.0 copy-done
  84.4 0.0 copy-start.4
  84.4 9.8 %fusion = bf16[768,6144]{1,0:T(8,128)(2,1)S(1)} fusion(bf16[1,768,6144]{2,1,0:T(8,128)(2,1)} %param.7, bf16[512,768]{1,0:T(8,128)(2,1)S(1)} %copy-done, bf16[512,6144]{0,1:T(8,128)(2,1)} %bitcast.29), kind=kOutput, calls=%fused_computation.1 | convolution fusion | flops 4845993984 | bytes 25952256 | tf_op jit(solution)/shard_map/dot_general | solution.py:25
  94.3 0.0 copy-start.1
  94.3 3.7 %copy-done.1 = bf16[768,6144]{1,0:T(8,128)(2,1)} copy-done((bf16[768,6144]{1,0:T(8,128)(2,1)}, bf16[768,6144]{1,0:T(8,128)(2,1)S(1)}, u32[]{:S(2)}) %copy-start.1) | copy-done | bytes 9437208
  98.0 0.0 copy-done.4
  98.0 3.6 %fusion.7 = f32[768,64]{0,1:T(8,128)} fusion(bf16[768,6144]{1,0:T(8,128)(2,1)S(1)} %fusion, bf16[6144,64]{0,1:T(8,128)(2,1)S(1)} %copy-done.4), kind=kOutput, calls=%fused_computation.17 | convolution fusion | flops 603979776 | bytes 10420224 | tf_op jit(solution)/shard_map/dot_general | solution.py:32
  101.7 0.0 all-reduce.3.cloned.1.call-update
  101.7 71.9 %all-reduce.3.cloned.1.call-done = f32[768,64]{0,1:T(8,128)} async-done(((f32[768,64]{0,1:T(8,128)}), f32[768,64]{0,1:T(8,128)}) %all-reduce.3.cloned.1.call-update) | async-done | bytes 196624 | tf_op jit(solution)/shard_map/psum | solution.py:33
  173.5 1.3 fusion.8
  174.9 10.3 %psum.22 = f32[64,64]{0,1:T(8,128)S(1)} all-reduce(f32[64,64]{0,1:T(8,128)S(1)} %fusion.8), channel_id=1, replica_groups=mesh['dp'=8,'mp'=4] {'mp'}, use_global_device_ids=true, to_apply=%region_1.0 | all-reduce | flops 4096 | bytes 32768 | tf_op jit(solution)/shard_map/psum | solution.py:40
  185.1 0.1 copy.12
  185.2 5.8 %cholesky.16 = f32[64,64]{1,0:T(8,128)S(1)} custom-call(f32[64,64]{1,0:T(8,128)S(1)} %fusion.5), custom_call_target="Cholesky" | custom-call | tf_op jit(solution)/shard_map/jit(cholesky)/cholesky | solution.py:41
  191.1 0.6 compare_reduce_fusion
  191.8 0.7 fusion.3
  192.4 4.9 %custom-call.7 = f32[1,64,64]{1,2,0:T(8,128)S(1)} custom-call(f32[1,64,64]{2,1,0:T(8,128)S(1)} %fusion.3), custom_call_target="InvertDiagBlocksLowerTriangular" | custom-call | tf_op jit(solution)/shard_map/jit(_solve_triangular)/triangular_solve | solution.py:42
  197.3 1.3 convolution_convert_fusion
  198.6 5.4 %fusion.9 = f32[6144,64]{0,1:T(8,128)S(1)} fusion(bf16[768,64]{0,1:T(8,128)(2,1)S(1)} %convolution_convert_fusion, bf16[768,6144]{1,0:T(8,128)(2,1)} %copy-done.1), kind=kOutput, calls=%fused_computation.19 | convolution fusion | flops 603979776 | bytes 11108352 | tf_op jit(solution)/shard_map/dot_general | solution.py:46
  204.1 55.9 %all-reduce.4 = bf16[6144,64]{0,1:T(8,128)(2,1)S(1)} all-reduce(f32[6144,64]{0,1:T(8,128)S(1)} %fusion.9), channel_id=1, replica_groups=mesh['dp'=8,'mp'=4] {'dp','mp'}, use_global_device_ids=true, to_apply=%region_4.5 | all-reduce | flops 393216 | bytes 2359296 | tf_op jit(solution)/shard_map/psum | solution.py:49
  259.9 0.0 copy-start.2
  260.0 0.0 copy-start.3
  260.0 7.8 %fusion.1 = bf16[1,768,6144]{2,1,0:T(8,128)(2,1)} fusion(bf16[768,64]{0,1:T(8,128)(2,1)S(1)} %convolution_convert_fusion, bf16[6144,64]{0,1:T(8,128)(2,1)S(1)} %all-reduce.4, bf16[768,6144]{1,0:T(8,128)(2,1)} %copy-done.1), kind=kOutput, calls=%fused_computation.3 | convolution fusion | flops 622854144 | bytes 19759104 | tf_op jit(solution)/shard_map/dot_general | solution.py:55
  267.8 0.0 copy-done.2
  267.8 0.0 copy-done.3
  267.8 1.9 multiply_add_fusion
  (2 shorter events, 0.0 us)
Async XLA Ops:
  7.2 77.3 %copy-start = (bf16[512,768]{1,0:T(8,128)(2,1)S(1)}, bf16[512,768]{1,0:T(8,128)(2,1)}, u32[]{:S(2)}) copy-start(bf16[512,768]{1,0:T(8,128)(2,1)} %param.5) | copy-start | bytes 2359300
  7.2 166.4 %all-reduce.3.cloned.1.call-start = ((), (), s32[]{:S(2)}) async-start(), calls=%async_computation.1 | async-start | bytes 393216 | tf_op jit(solution)/shard_map/psum | solution.py:33
  84.4 13.6 %copy-start.4 = (bf16[6144,64]{0,1:T(8,128)(2,1)S(1)}, bf16[6144,64]{0,1:T(8,128)(2,1)}, u32[]{:S(2)}) copy-start(bf16[6144,64]{0,1:T(8,128)(2,1)} %param.8) | copy-start | bytes 2359300
  94.3 3.7 %copy-start.1 = (bf16[768,6144]{1,0:T(8,128)(2,1)}, bf16[768,6144]{1,0:T(8,128)(2,1)S(1)}, u32[]{:S(2)}) copy-start(bf16[768,6144]{1,0:T(8,128)(2,1)S(1)} %fusion) | copy-start | bytes 28311556
  259.9 7.8 %copy-start.2 = (bf16[6144,64]{0,1:T(8,128)(2,1)}, bf16[6144,64]{0,1:T(8,128)(2,1)S(1)}, u32[]{:S(2)}) copy-start(bf16[6144,64]{0,1:T(8,128)(2,1)S(1)} %all-reduce.4) | copy-start | bytes 2359300
  260.0 7.8 %copy-start.3 = (f32[768,768]{1,0:T(8,128)S(1)}, f32[768,768]{1,0:T(8,128)}, u32[]{:S(2)}) copy-start(f32[768,768]{1,0:T(8,128)} %param.9) | copy-start | bytes 7077892
Sparse Core Ops, SparseCore 0:
  101.8 71.6 all-reduce.2
